TPU v7x, 128 devices: a whole 4x4x4 slice. The times are simulated.
128 devices in a mesh: variant: 8 (over z_lo, x), vocab: 16 (over y, z_hi, core).
Axes of the slice: x: 4, y: 4, z: 4 (z_hi: 2, z_lo: 2; z = z_hi * 2 + z_lo), core: 2. Of those that a mesh axis runs over, the one named last changes fastest.
Arguments:
- teacher_hidden: bfloat16 [8, 256, 4096], P(None, None, ('variant', 'vocab')), may hold values from -24 to 24
- teacher_weight: bfloat16 [4096, 64128], P(None, ('vocab', 'variant')), may hold values from -1 to 1
- variant_ids: int32 [8], replicated, may hold values from 0 to 13
- temps: float32 [14], replicated, may hold values from 0.7 to 1.5
- student_hidden: bfloat16 [256, 2048], P(None, 'variant'), may hold values from -24 to 24
- student_weight: bfloat16 [2048, 64128], P('variant', 'vocab'), may hold values from -1 to 1
- token_ids: int32 [256], P('variant'), may hold values from 0 to 64127
- loss_mask: int32 [256], P('variant'), may hold values 0 or 1
Outputs:
- token_loss: float32 [256], P('variant')
- student_grad: float32 [2048, 64128], P('variant', 'vocab')
All inputs are finite; a program needn't handle non-finite values. No bound on the sum of `loss_mask` on one device may be relied on, other than what follows from the above.
Results may differ from a plain program's by a relative error of at most 0.0025.
Values may be sent and summed in bfloat16 or wider, within the bound.
No kernel may reach another device: no remote copies, remote signals or barrier semaphores. Data moves between devices by JAX's collectives and lax.ppermute only.
A program may use at most 192 MiB of HBM per device.

v0:
```python
import jax
import jax.numpy as jnp
from jax import lax
from jax.sharding import PartitionSpec as P

mix_weight = 0.5
loss_scale = 4096.0


def on_device(
    teacher_hidden,
    teacher_weight,
    variant_ids,
    temps,
    student_hidden,
    student_weight,
    token_ids,
    loss_mask,
):
    n_variant = lax.axis_size("variant")
    categories = jnp.arange(temps.shape[0], dtype=jnp.int32)
    taus = jnp.sum(
        jnp.where(variant_ids[:, None] == categories[None, :], temps[None, :], 0.0), axis=1
    )
    hidden_all = lax.all_gather(teacher_hidden, ("variant", "vocab"), axis=2, tiled=True)
    scaled = (
        jnp.einsum("vtd,dc->vtc", hidden_all, teacher_weight, preferred_element_type=jnp.float32)
        / taus[:, None, None]
    )
    local_max = jnp.max(scaled, axis=2)
    top = lax.pmax(local_max, ("variant", "vocab"))
    total = lax.psum(jnp.sum(jnp.exp(scaled - top[:, :, None]), axis=2), ("variant", "vocab"))
    probs = jnp.exp(scaled - top[:, :, None]) / total[:, :, None]
    averaged_cols = jnp.sum(probs, axis=0) / n_variant
    averaged = lax.all_to_all(
        averaged_cols.astype(jnp.bfloat16), "variant", split_axis=0, concat_axis=1, tiled=True
    ).astype(averaged_cols.dtype)
    block = student_hidden
    logits = lax.psum_scatter(
        jnp.dot(block, student_weight, preferred_element_type=jnp.float32),
        "variant",
        scatter_dimension=0,
        tiled=True,
    )
    local_max = jnp.max(logits, axis=1)
    top = lax.pmax(local_max, "vocab")
    total = lax.psum(jnp.sum(jnp.exp(logits - top[:, None]), axis=1), "vocab")
    log_probs = logits - (top + jnp.log(total))[:, None]
    probs_student = jnp.exp(log_probs)
    columns = lax.axis_index("vocab") * logits.shape[1] + jnp.arange(
        logits.shape[1], dtype=jnp.int32
    )
    onehot = token_ids[:, None] == columns[None, :]
    soft, hard = lax.psum(
        (jnp.sum(averaged * log_probs, axis=1), jnp.sum(jnp.where(onehot, log_probs, 0.0), axis=1)),
        "vocab",
    )
    maskf = loss_mask.astype(jnp.float32)
    token_loss = maskf * (-mix_weight * soft - (1.0 - mix_weight) * hard)
    error = (
        loss_scale
        * maskf[:, None]
        * (probs_student - mix_weight * averaged - (1.0 - mix_weight) * onehot.astype(jnp.float32))
    ).astype(jnp.bfloat16)
    block = student_hidden
    student_grad = lax.dot_general(
        block,
        lax.all_gather(error, "variant", axis=0, tiled=True),
        (((0,), (0,)), ((), ())),
        preferred_element_type=jnp.float32,
    )
    return (token_loss, student_grad)


def solution(mesh):
    in_specs = (
        P(None, None, ("variant", "vocab")),
        P(None, ("vocab", "variant")),
        P(),
        P(),
        P(None, "variant"),
        P("variant", "vocab"),
        P("variant"),
        P("variant"),
    )
    out_specs = (P("variant"), P("variant", "vocab"))
    return jax.shard_map(
        on_device, mesh=mesh, in_specs=in_specs, out_specs=out_specs, check_vma=False
    )
```

profile of v0, /device:TPU:0, one launch (start us, length us, event | category | flops | bytes accessed | tf_op | source)
XLA Modules:
  0.0 505.8 jit_solution(16824957268856968234)
XLA Ops:
  8.0 0.0 copy-start
  8.0 0.0 copy-start.5
  8.0 0.0 copy-start.6
  8.0 0.0 copy-start.4
  8.0 0.0 reduce-scatter.2.cloned.1.call-start
  8.1 1.5 copy-done
  9.6 3.6 fusion.11
  13.2 0.0 reduce-scatter.2.cloned.1.call-update
  13.2 0.0 all-gather.3.cloned.1.call-start
  13.2 0.5 all-gather.3.cloned.1.call-update
  13.8 0.0 copy-done.5
  13.8 0.0 copy-done.6
  13.8 0.2 select_reduce_fusion
  14.0 0.0 copy-done.4
  14.0 60.6 %reduce-scatter.2.cloned.1.call-done = f32[32,4008]{1,0:T(8,128)} async-done(((f32[256,4008]{1,0:T(8,128)}), f32[32,4008]{1,0:T(8,128)}) %reduce-scatter.2.cloned.1.call-update) | async-done | bytes 513040 | tf_op jit(solution)/shard_map/reduce_scatter | solution.py:39
  74.6 1.2 reduce_max.19
  75.8 38.9 %pmax.15 = f32[32]{0:T(128)S(1)} all-reduce(f32[32]{0:T(128)S(1)} %reduce_max.19), channel_id=1, replica_groups=mesh['variant'=8,'vocab'=16] {'vocab'}, use_global_device_ids=true, to_apply=%region_8.9 | all-reduce | flops 32 | bytes 256 | tf_op jit(solution)/shard_map/pmax | solution.py:46
  114.7 151.1 %all-gather.3.cloned.1.call-done = bf16[8,256,4096]{1,2,0:T(8,128)(2,1)} async-done(((bf16[8,256,32]{1,2,0:T(8,128)(2,1)}), bf16[8,256,4096]{1,2,0:T(8,128)(2,1)}) %all-gather.3.cloned.1.call-update) | async-done | bytes 16777232 | tf_op jit(solution)/shard_map/all_gather | solution.py:25
  265.9 14.8 %fusion.10 = (f32[8,256]{1,0:T(8,128)S(1)}, f32[8,256,501]{1,2,0:T(8,128)}) fusion(f32[8]{0:T(128)S(1)} %select_reduce_fusion, bf16[8,256,4096]{1,2,0:T(8,128)(2,1)} %all-gather.3.cloned.1.call-done, bf16[4096,501]{0,1:T(8,128)(2,1)} %param.9), kind=kOutput, calls=%fused_computation.23 | convolution fusion | flops 8407435264 | bytes 24993824 | tf_op jit(solution)/shard_map/vtd,dc->vtc/dot_general | solution.py:27
  280.6 62.0 %pmax.14 = f32[8,256]{1,0:T(8,128)S(1)} all-reduce(f32[8,256]{1,0:T(8,128)S(1)} %get-tuple-element.7), channel_id=1, replica_groups=mesh['variant'=8,'vocab'=16] {'variant','vocab'}, use_global_device_ids=true, to_apply=%region_2.3 | all-reduce | flops 2048 | bytes 16384 | tf_op jit(solution)/shard_map/pmax | solution.py:31
  342.6 2.7 fusion.2
  345.4 0.0 copy-start.1
  345.4 64.6 %psum.28 = f32[8,256]{1,0:T(8,128)S(1)} all-reduce(f32[8,256]{1,0:T(8,128)S(1)} %fusion.2), channel_id=1, replica_groups=mesh['variant'=8,'vocab'=16] {'variant','vocab'}, use_global_device_ids=true, to_apply=%region_4.5 | all-reduce | flops 2048 | bytes 16384 | tf_op jit(solution)/shard_map/psum | solution.py:32
  410.0 0.0 copy-start.3
  410.0 2.9 divide_reduce_fusion
  412.9 0.0 copy-start.2
  413.0 0.8 copy.13
  413.8 3.4 all-to-all-start
  417.3 0.0 all-gather.5.cloned.1.call-start
  417.3 0.0 copy-done.1
  417.3 0.3 exponential_reduce_fusion
  417.6 34.1 %psum.29 = f32[32]{0:T(128)S(1)} all-reduce(f32[32]{0:T(128)S(1)} %exponential_reduce_fusion), channel_id=1, replica_groups=mesh['variant'=8,'vocab'=16] {'vocab'}, use_global_device_ids=true, to_apply=%region_10.11 | all-reduce | flops 32 | bytes 256 | tf_op jit(solution)/shard_map/psum | solution.py:47
  451.7 0.0 all-to-all-done
  451.7 0.1 convert_bitcast_fusion
  451.8 1.1 copy.14
  452.9 1.4 reshape.27
  454.2 0.0 copy-done.3
  454.2 1.1 multiply_reduce_fusion
  455.4 0.0 all-gather.5.cloned.1.call-update
  455.4 33.7 %all-reduce = (f32[32]{0:T(128)S(1)}, f32[32]{0:T(128)S(1)}) all-reduce(f32[32]{0:T(128)S(1)} %get-tuple-element.3, f32[32]{0:T(128)S(1)} %get-tuple-element.2), channel_id=1, replica_groups=mesh['variant'=8,'vocab'=16] {'vocab'}, use_global_device_ids=true, to_apply=%region_14.15 | all-reduce | flops 64 | bytes 512 | tf_op jit(solution)/shard_map/psum | solution.py:54
  489.1 0.5 subtract_multiply_fusion
  489.6 4.4 all-gather.5.cloned.1.call-done
  494.0 0.0 copy-done.2
  494.0 4.3 convolution_bitcast_fusion
  (4 shorter events, 0.1 us)
Async XLA Ops:
  8.0 1.6 copy-start
  8.0 5.8 %copy-start.5 = (f32[14]{0:T(128)S(1)}, f32[14]{0:T(128)}, u32[]{:S(2)}) copy-start(f32[14]{0:T(128)} %param.11) | copy-start | bytes 172
  8.0 5.8 %copy-start.6 = (s32[8]{0:T(128)S(1)}, s32[8]{0:T(128)}, u32[]{:S(2)}) copy-start(s32[8]{0:T(128)} %param.10) | copy-start | bytes 100
  8.0 5.9 %copy-start.4 = (s32[32]{0:T(128)S(1)}, s32[32]{0:T(128)}, u32[]{:S(2)}) copy-start(s32[32]{0:T(128)} %param.15) | copy-start | bytes 388
  8.0 66.6 %reduce-scatter.2.cloned.1.call-start = ((), (), s32[]{:S(2)}) async-start(), calls=%async_computation.3 | async-start | bytes 4718592 | tf_op jit(solution)/shard_map/reduce_scatter | solution.py:39
  13.2 252.7 %all-gather.3.cloned.1.call-start = ((), (), s32[]{:S(2)}) async-start(), calls=%async_computation.2 | async-start | bytes 16908288 | tf_op jit(solution)/shard_map/all_gather | solution.py:25
  345.4 71.9 %copy-start.1 = (f32[32,4008]{1,0:T(8,128)S(1)}, f32[32,4008]{1,0:T(8,128)}, u32[]{:S(2)}) copy-start(f32[32,4008]{1,0:T(8,128)} %reduce-scatter.2.cloned.1.call-done) | copy-start | bytes 1539076
  410.0 44.2 %copy-start.3 = (s32[32]{0:T(128)S(1)}, s32[32]{0:T(128)}, u32[]{:S(2)}) copy-start(s32[32]{0:T(128)} %param.14) | copy-start | bytes 388
  412.9 81.1 %copy-start.2 = (bf16[256,256]{1,0:T(8,128)(2,1)S(1)}, bf16[256,256]{1,0:T(8,128)(2,1)}, u32[]{:S(2)}) copy-start(bf16[256,256]{1,0:T(8,128)(2,1)} %param.12) | copy-start | bytes 393220
  413.8 37.9 %all-to-all-start = ((bf16[8,32,501]{2,1,0:T(8,128)(2,1)}), bf16[8,32,501]{2,1,0:T(8,128)(2,1)S(1)}, u32[]{:S(2)}, u32[]{:S(2)}) async-start(bf16[8,32,501]{2,1,0:T(8,128)(2,1)} %bitcast.1), calls=%async_computation | async-start | bytes 524288 | tf_op jit(solution)/shard_map/all_to_all | solution.py:35
  417.3 76.8 %all-gather.5.cloned.1.call-start = ((), (), s32[]{:S(2)}) async-start(), calls=%async_computation.4 | async-start | bytes 2359296 | tf_op jit(solution)/shard_map/all_gather | solution.py:68
Sparse Core Ops, SparseCore 0:
  13.3 61.2 reduce-scatter.1
  455.5 38.4 all-gather.4
Sparse Core Ops, SparseCore 1:
  15.4 250.4 all-gather.2
where the time goes:
time: 506 us
  blocking collectives  233 us (46%)
  waiting for transfers between devices  217 us (43%)
  matrix products  22.7 us (4%)
  between operations  15.6 us (3%)
  other arithmetic  9.06 us (2%)
    all_gather x1, waiting for transfers between devices, on_device(): lax.all_gather(teacher_hidden, ('variant', 'vocab'), axis=2, tiled=True)  151 us
    psum x1, blocking collectives, on_device(): lax.psum(jnp.sum(jnp.exp(scaled - top[:, :, None]), axis=2), ('variant',...  64.6 us
    pmax x1, blocking collectives, on_device(): top = lax.pmax(local_max, ('variant', 'vocab'))  62 us
    reduce_scatter x1, waiting for transfers between devices, on_device(): lax.psum_scatter(jnp.dot(block, student_weight, preferred_element_type=jn...  60.6 us
    pmax x1, blocking collectives, on_device(): top = lax.pmax(local_max, 'vocab')  38.9 us
    psum x1, blocking collectives, on_device(): total = lax.psum(jnp.sum(jnp.exp(logits - top[:, None]), axis=1), 'vocab')  34.1 us
    psum x1, blocking collectives, on_device(): lax.psum((jnp.sum(averaged * log_probs, axis=1), jnp.sum(jnp.where(onehot...  33.7 us
    dot_general x1, matrix products, on_device(): jnp.einsum('vtd,dc->vtc', hidden_all, teacher_weight, preferred_element_t...  14.8 us
  transfers between devices with their start and end apart: 4, of which 3 were waited for; matrix products, arithmetic and copies ran while one was open for 0% of the time, Pallas kernels for 0%

commit v1 on v0

--- a/solution.py
+++ b/solution.py
@@ -44,7 +44,9 @@
     )
     local_max = jnp.max(logits, axis=1)
     top = lax.pmax(local_max, "vocab")
-    total = lax.psum(jnp.sum(jnp.exp(logits - top[:, None]), axis=1), "vocab")
+    total = jnp.sum(
+        lax.all_gather(jnp.sum(jnp.exp(logits - top[:, None]), axis=1), "vocab"), axis=0
+    )
     log_probs = logits - (top + jnp.log(total))[:, None]
     probs_student = jnp.exp(log_probs)
     columns = lax.axis_index("vocab") * logits.shape[1] + jnp.arange(

time: 506 us -> 506 us (level)
    unnamed x0 -> x1, blocking collectives: none -> 34.1 us
    psum x1 -> x0, blocking collectives: 34.1 us -> none  [on_device(): total = lax.psum(jnp.sum(jnp.exp(logits - top[:, None]), axis=1), 'vocab')]
  transfers between devices with their start and end apart: 4 -> 4, of which waited for: 3 -> 3; matrix products, arithmetic and copies ran while one was open for 0% -> 1% of each run, Pallas kernels for 0% -> 0%
where the time goes in v1:
time: 506 us
  blocking collectives  234 us (46%)
  waiting for transfers between devices  214 us (42%)
  matrix products  22.7 us (4%)
  between operations  16.3 us (3%)
  other arithmetic  10.2 us (2%)
  local copies, waits for them, and re-layouts  5.73 us (1%)
    all_gather x1, waiting for transfers between devices, on_device(): lax.all_gather(teacher_hidden, ('variant', 'vocab'), axis=2, tiled=True)  149 us
    psum x1, blocking collectives, on_device(): lax.psum(jnp.sum(jnp.exp(scaled - top[:, :, None]), axis=2), ('variant',...  64.6 us
    pmax x1, blocking collectives, on_device(): top = lax.pmax(local_max, ('variant', 'vocab'))  62.3 us
    reduce_scatter x1, waiting for transfers between devices, on_device(): lax.psum_scatter(jnp.dot(block, student_weight, preferred_element_type=jn...  59.4 us
    pmax x1, blocking collectives, on_device(): top = lax.pmax(local_max, 'vocab')  38.9 us
    unnamed x1, blocking collectives  34.1 us
    psum x1, blocking collectives, on_device(): lax.psum((jnp.sum(averaged * log_probs, axis=1), jnp.sum(jnp.where(onehot...  33.7 us
    dot_general x1, matrix products, on_device(): jnp.einsum('vtd,dc->vtc', hidden_all, teacher_weight, preferred_element_t...  14.8 us
  transfers between devices with their start and end apart: 4, of which 3 were waited for; matrix products, arithmetic and copies ran while one was open for 1% of the time, Pallas kernels for 0%

profile of v1, /device:TPU:0, one launch (start us, length us, event | category | flops | bytes accessed | tf_op | source)
XLA Modules:
  0.0 505.6 jit_solution(6001449348035575898)
XLA Ops:
  8.0 0.0 copy-start
  8.0 0.0 copy-start.7
  8.0 0.0 copy-start.5
  8.0 0.0 copy-start.6
  8.0 0.0 copy-start.4
  8.1 0.0 reduce-scatter.2.cloned.1.call-start
  8.1 1.5 copy-done
  9.6 3.6 fusion.11
  13.2 0.0 reduce-scatter.2.cloned.1.call-update
  13.2 0.0 all-gather.4.cloned.1.call-start
  13.2 0.5 all-gather.4.cloned.1.call-update
  13.8 0.0 copy-done.7
  13.8 0.6 dynamic-slice
  15.0 0.0 copy-done.5
  15.0 0.0 copy-done.6
  15.0 0.2 select_reduce_fusion
  15.2 0.0 copy-done.4
  15.2 59.4 %reduce-scatter.2.cloned.1.call-done = f32[32,4008]{1,0:T(8,128)} async-done(((f32[256,4008]{1,0:T(8,128)}), f32[32,4008]{1,0:T(8,128)}) %reduce-scatter.2.cloned.1.call-update) | async-done | bytes 513040 | tf_op jit(solution)/shard_map/reduce_scatter | solution.py:39
  74.6 1.2 reduce_max.19
  75.8 38.9 %pmax.15 = f32[32]{0:T(128)S(1)} all-reduce(f32[32]{0:T(128)S(1)} %reduce_max.19), channel_id=1, replica_groups=mesh['variant'=8,'vocab'=16] {'vocab'}, use_global_device_ids=true, to_apply=%region_8.9 | all-reduce | flops 32 | bytes 256 | tf_op jit(solution)/shard_map/pmax | solution.py:46
  114.7 1.3 exponential_reduce_fusion
  116.0 0.2 dynamic-update-slice
  116.3 149.2 %all-gather.4.cloned.1.call-done = bf16[8,256,4096]{1,2,0:T(8,128)(2,1)} async-done(((bf16[8,256,32]{1,2,0:T(8,128)(2,1)}), bf16[8,256,4096]{1,2,0:T(8,128)(2,1)}) %all-gather.4.cloned.1.call-update) | async-done | bytes 16777232 | tf_op jit(solution)/shard_map/all_gather | solution.py:25
  265.5 14.8 %fusion.10 = (f32[8,256]{1,0:T(8,128)S(1)}, f32[8,256,501]{1,2,0:T(8,128)}) fusion(f32[8]{0:T(128)S(1)} %select_reduce_fusion, bf16[8,256,4096]{1,2,0:T(8,128)(2,1)} %all-gather.4.cloned.1.call-done, bf16[4096,501]{0,1:T(8,128)(2,1)} %param.9), kind=kOutput, calls=%fused_computation.23 | convolution fusion | flops 8407435264 | bytes 24993824 | tf_op jit(solution)/shard_map/vtd,dc->vtc/dot_general | solution.py:27
  280.2 62.3 %pmax.14 = f32[8,256]{1,0:T(8,128)S(1)} all-reduce(f32[8,256]{1,0:T(8,128)S(1)} %get-tuple-element.7), channel_id=1, replica_groups=mesh['variant'=8,'vocab'=16] {'variant','vocab'}, use_global_device_ids=true, to_apply=%region_2.3 | all-reduce | flops 2048 | bytes 16384 | tf_op jit(solution)/shard_map/pmax | solution.py:31
  342.5 2.7 fusion.2
  345.3 64.6 %psum.21 = f32[8,256]{1,0:T(8,128)S(1)} all-reduce(f32[8,256]{1,0:T(8,128)S(1)} %fusion.2), channel_id=1, replica_groups=mesh['variant'=8,'vocab'=16] {'variant','vocab'}, use_global_device_ids=true, to_apply=%region_4.5 | all-reduce | flops 2048 | bytes 16384 | tf_op jit(solution)/shard_map/psum | solution.py:32
  409.9 0.0 copy-start.1
  409.9 3.0 divide_reduce_fusion
  412.9 0.0 copy-start.2
  413.0 0.8 copy.13
  413.8 3.4 all-to-all-start
  417.2 0.0 all-gather.6.cloned.1.call-start
  417.3 34.1 %all-reduce = f32[512]{0:T(512)S(1)} all-reduce(f32[512]{0:T(512)S(1)} %dynamic-update-slice), channel_id=2, replica_groups=mesh['variant'=8,'vocab'=16] {'vocab'}, use_global_device_ids=true, to_apply=%add | all-reduce | flops 512 | bytes 4096
  451.4 0.1 reshape.28
  451.5 0.0 all-to-all-done
  451.5 0.1 convert_bitcast_fusion
  451.6 1.1 copy.14
  452.7 1.4 reshape.27
  454.1 0.0 copy-done.1
  454.1 0.0 copy-done.3
  454.1 1.1 multiply_reduce_fusion
  455.2 0.0 all-gather.6.cloned.1.call-update
  455.2 33.7 %all-reduce.1 = (f32[32]{0:T(128)S(1)}, f32[32]{0:T(128)S(1)}) all-reduce(f32[32]{0:T(128)S(1)} %get-tuple-element.3, f32[32]{0:T(128)S(1)} %get-tuple-element.2), channel_id=1, replica_groups=mesh['variant'=8,'vocab'=16] {'vocab'}, use_global_device_ids=true, to_apply=%region_14.15 | all-reduce | flops 64 | bytes 512 | tf_op jit(solution)/shard_map/psum | solution.py:56
  488.9 0.5 subtract_multiply_fusion
  489.4 4.4 all-gather.6.cloned.1.call-done
  493.8 0.0 copy-done.2
  493.8 4.3 convolution_bitcast_fusion
  (7 shorter events, 0.1 us)
Async XLA Ops:
  8.0 1.6 copy-start
  8.0 5.8 %copy-start.7 = (u32[128]{0:T(128)S(1)}, u32[128]{0:T(128)}, u32[]{:S(2)}) copy-start(u32[128]{0:T(128)} %constant.26) | copy-start | bytes 1540
  8.0 7.0 %copy-start.5 = (f32[14]{0:T(128)S(1)}, f32[14]{0:T(128)}, u32[]{:S(2)}) copy-start(f32[14]{0:T(128)} %param.11) | copy-start | bytes 172
  8.0 7.0 %copy-start.6 = (s32[8]{0:T(128)S(1)}, s32[8]{0:T(128)}, u32[]{:S(2)}) copy-start(s32[8]{0:T(128)} %param.10) | copy-start | bytes 100
  8.0 7.2 %copy-start.4 = (s32[32]{0:T(128)S(1)}, s32[32]{0:T(128)}, u32[]{:S(2)}) copy-start(s32[32]{0:T(128)} %param.15) | copy-start | bytes 388
  8.1 66.5 %reduce-scatter.2.cloned.1.call-start = ((), (), s32[]{:S(2)}) async-start(), calls=%async_computation.3 | async-start | bytes 4718592 | tf_op jit(solution)/shard_map/reduce_scatter | solution.py:39
  13.2 252.3 %all-gather.4.cloned.1.call-start = ((), (), s32[]{:S(2)}) async-start(), calls=%async_computation.2 | async-start | bytes 16908288 | tf_op jit(solution)/shard_map/all_gather | solution.py:25
  409.9 44.2 %copy-start.1 = (f32[32,4008]{1,0:T(8,128)S(1)}, f32[32,4008]{1,0:T(8,128)}, u32[]{:S(2)}) copy-start(f32[32,4008]{1,0:T(8,128)} %reduce-scatter.2.cloned.1.call-done) | copy-start | bytes 1539076
  409.9 44.2 %copy-start.3 = (s32[32]{0:T(128)S(1)}, s32[32]{0:T(128)}, u32[]{:S(2)}) copy-start(s32[32]{0:T(128)} %param.14) | copy-start | bytes 388
  412.9 80.9 %copy-start.2 = (bf16[256,256]{1,0:T(8,128)(2,1)S(1)}, bf16[256,256]{1,0:T(8,128)(2,1)}, u32[]{:S(2)}) copy-start(bf16[256,256]{1,0:T(8,128)(2,1)} %param.12) | copy-start | bytes 393220
  413.8 37.7 %all-to-all-start = ((bf16[8,32,501]{2,1,0:T(8,128)(2,1)}), bf16[8,32,501]{2,1,0:T(8,128)(2,1)S(1)}, u32[]{:S(2)}, u32[]{:S(2)}) async-start(bf16[8,32,501]{2,1,0:T(8,128)(2,1)} %bitcast.1), calls=%async_computation | async-start | bytes 524288 | tf_op jit(solution)/shard_map/all_to_all | solution.py:35
  417.2 76.6 %all-gather.6.cloned.1.call-start = ((), (), s32[]{:S(2)}) async-start(), calls=%async_computation.4 | async-start | bytes 2359296 | tf_op jit(solution)/shard_map/all_gather | solution.py:70
Sparse Core Ops, SparseCore 0:
  13.3 61.2 reduce-scatter.1
  455.4 38.4 all-gather.5
Sparse Core Ops, SparseCore 1:
  15.4 250.0 all-gather.3
